TPU v7x, 256 devices: a whole 4x4x8 slice. The times are simulated.
256 devices in a mesh: tp: 8 (over y, core), ep: 32 (over z, x).
Axes of the slice: x: 4, y: 4, z: 8, core: 2. Of those that a mesh axis runs over, the one named last changes fastest.
Arguments:
- tokens: bfloat16 [512, 8192], P('ep'), may hold values from -6 to 6
- cotangent: bfloat16 [512, 8192], P('ep'), may hold values from -6 to 6
- w_gate: bfloat16 [14336, 8192], P(('tp', 'ep')), may hold values from -0.0625 to 0.0625
- w_up: bfloat16 [14336, 8192], P(('tp', 'ep')), may hold values from -0.0625 to 0.0625
- w_down: bfloat16 [14336, 8192], P(('tp', 'ep')), may hold values from -0.375 to 0.375
- neuron_expert: int32 [14336], P(('tp', 'ep')), may hold values from 0 to 63, as said below
- neuron_slot: int32 [14336], P(('tp', 'ep')), may hold values from 0 to 63, as said below
- choice_expert: int32 [512, 8], P('ep'), may hold values from 0 to 63, all different within a row; in each aligned block of 16 rows (0 to 15, 16 to 31, ...) at most 4 rows name the same one
- choice_weight: float32 [512, 8], P('ep'), may hold values from 0.02 to 0.3
Outputs:
- output: bfloat16 [512, 8192], P('ep', 'tp')
- d_tokens: bfloat16 [512, 8192], P('ep', 'tp')
- d_weight: float32 [512, 8], P('ep')
- d_gate_exp: bfloat16 [64, 512, 8192], P('ep', 'tp')
- d_up_exp: bfloat16 [64, 512, 8192], P('ep', 'tp')
- d_down_exp: bfloat16 [64, 512, 8192], P('ep', 'tp')
Inputs may be any that keep to these rules, and one draw needn't show every extreme that they name: `neuron_expert`: expert e belongs to ep index e // 2. Among the 56 neurons starting at any multiple of 56, at most 4 name experts of one ep index. `neuron_slot`: within each tp range of 1792 neurons, the neurons of one expert have distinct slots. `choice_expert`: each row names 8 different experts; in each aligned block of 16 rows no expert is named more than 4 times.
All inputs are finite; a program needn't handle non-finite values.
Results may differ from a plain program's by a relative error of at most 0.018.
Values may be sent and summed in bfloat16 or wider, within the bound.
No kernel may reach another device: no remote copies, remote signals or barrier semaphores. Data moves between devices by JAX's collectives and lax.ppermute only.
A program may use at most 128 MiB of HBM per device.

v0:
```python
import jax
import jax.numpy as jnp
from jax import lax
from jax.sharding import PartitionSpec as P

NL = 56
E_DEV = 2
TOPK = 8


def earlier_same(labels):
    count = labels.shape[0]
    row_iota = lax.broadcasted_iota(jnp.int32, (count, count), 0)
    col_iota = lax.broadcasted_iota(jnp.int32, (count, count), 1)
    same = (labels[:, None] == labels[None, :]) & (col_iota < row_iota)
    return jnp.sum(same.astype(jnp.int32), 1)


def slope_of(gate):
    sig = jax.nn.sigmoid(gate)
    return sig * (1.0 + gate * (1.0 - sig))


def source_table(matches):
    column = lax.broadcasted_iota(jnp.int32, matches.shape, 1)
    index = jnp.sum(jnp.where(matches, column, 0), 1)
    return (index, jnp.any(matches, 1))


def pick_rows(rows, index, filled):
    taken = jnp.take(rows, index, axis=0)
    return jnp.where(filled[:, None], taken, jnp.zeros_like(taken))


def dispatch(rows):
    return lax.all_to_all(rows, "ep", split_axis=0, concat_axis=0, tiled=True)


def to_sources(terms, n_ep, tcap):
    shares = []
    for term in terms:
        share = lax.psum_scatter(term.astype(jnp.bfloat16), "tp", scatter_dimension=1, tiled=True)
        shares.append(share.reshape(n_ep, tcap, -1))
    stacked = jnp.stack(shares, 1).reshape(n_ep, E_DEV * tcap, -1)
    moved = lax.all_to_all(stacked, "ep", split_axis=0, concat_axis=0, tiled=True)
    return moved.reshape(-1, stacked.shape[2])


def body(
    tokens,
    cotangent,
    w_gate,
    w_up,
    w_down,
    neuron_expert,
    neuron_slot,
    choice_expert,
    choice_weight,
):
    n_ep = lax.axis_size("ep")
    n_tp = lax.axis_size("tp")
    width = tokens.shape[1]
    local_width = width // n_tp
    peer_slots = 2 * ((NL + n_ep - 1) // n_ep)
    capacity = n_ep * peer_slots // E_DEV
    owner = neuron_expert // E_DEV
    target = owner * peer_slots + earlier_same(owner)
    packing = target[None, :] == jnp.arange(n_ep * peer_slots, dtype=jnp.int32)[:, None]
    pack_index, pack_filled = source_table(packing)
    labels = neuron_expert % E_DEV * capacity + neuron_slot + 1
    packed_labels = jnp.sum(jnp.where(packing, labels[None, :], 0), 1)
    packed_labels = packed_labels.astype(jnp.float32).astype(jnp.bfloat16).reshape(n_ep, peer_slots)

    def pack(weight):
        return pick_rows(weight, pack_index, pack_filled).reshape(n_ep, peer_slots, width)

    got_gate, got_up, got_down, got_labels = (
        lax.all_to_all(pack(w_gate), "ep", split_axis=0, concat_axis=0, tiled=True),
        lax.all_to_all(pack(w_up), "ep", split_axis=0, concat_axis=0, tiled=True),
        lax.all_to_all(pack(w_down), "ep", split_axis=0, concat_axis=0, tiled=True),
        lax.all_to_all(packed_labels, "ep", split_axis=0, concat_axis=0, tiled=True),
    )
    slot_of = got_labels.reshape(-1).astype(jnp.int32) - 1
    placing = slot_of[None, :] == jnp.arange(E_DEV * capacity, dtype=jnp.int32)[:, None]
    place_index, place_filled = source_table(placing)

    def place(rows):
        return pick_rows(rows.reshape(-1, width), place_index, place_filled).reshape(
            E_DEV, capacity, width
        )

    gate_exp = place(got_gate)
    up_exp = place(got_up)
    down_exp = place(got_down)
    tok_dev = tokens.shape[0]
    chosen = choice_expert.reshape(-1)
    count = chosen.shape[0]
    experts_all = E_DEV * n_ep
    tcap = max(2, 2 * count // experts_all)
    slot_ids = chosen * tcap + earlier_same(chosen)
    matching = slot_ids[None, :] == jnp.arange(experts_all * tcap, dtype=jnp.int32)[:, None]
    choice_of_slot, slot_used = source_table(matching)
    send_x = pick_rows(tokens, choice_of_slot // TOPK, slot_used)
    send_x = send_x.reshape(n_ep, E_DEV * tcap, width)
    x_got = dispatch(send_x).reshape(n_ep, E_DEV, tcap, width)
    saved = []
    terms = []
    for local in range(E_DEV):
        x_rows = x_got[:, local].reshape(-1, width)
        gate = jnp.einsum("rd,hd->rh", x_rows, gate_exp[local], preferred_element_type=jnp.float32)
        upper = jnp.einsum("rd,hd->rh", x_rows, up_exp[local], preferred_element_type=jnp.float32)
        hidden = (jax.nn.silu(gate) * upper).astype(jnp.bfloat16)
        terms.append(jnp.dot(hidden, down_exp[local], preferred_element_type=jnp.float32))
        saved.append((x_rows, gate, upper, hidden))
    results = to_sources(terms, n_ep, tcap)
    per_choice = jnp.take(results, slot_ids, axis=0).astype(jnp.float32)
    weights = choice_weight.reshape(-1, 1)
    output = jnp.sum((weights * per_choice).reshape(tok_dev, TOPK, local_width), 1).astype(
        jnp.bfloat16
    )
    cot_local = lax.dynamic_slice_in_dim(
        cotangent, lax.axis_index("tp") * local_width, local_width, 1
    ).astype(jnp.float32)
    partial_value = jnp.sum(
        per_choice.reshape(tok_dev, TOPK, local_width) * cot_local[:, None, :], 2
    )
    d_weight = lax.psum(partial_value, "tp")
    slot_weight = jnp.take(choice_weight.reshape(-1), choice_of_slot, axis=0)
    slot_cot = jnp.take(cotangent, choice_of_slot // TOPK, axis=0).astype(jnp.float32)
    scaled_rows = (slot_weight[:, None] * slot_cot).astype(jnp.bfloat16)
    send_g = jnp.where(slot_used[:, None], scaled_rows, jnp.zeros_like(scaled_rows))
    send_g = send_g.reshape(n_ep, E_DEV * tcap, width)
    g_got = dispatch(send_g).reshape(n_ep, E_DEV, tcap, width)
    grad_gate = []
    grad_up = []
    grad_down = []
    back_terms = []
    for local in range(E_DEV):
        x_rows, gate, upper, hidden = saved[local]
        g_rows = g_got[:, local].reshape(-1, width)
        d_hidden = jnp.einsum(
            "rd,hd->rh", g_rows, down_exp[local], preferred_element_type=jnp.float32
        )
        grad_down.append(
            jnp.einsum("rh,rd->hd", hidden, g_rows, preferred_element_type=jnp.float32).astype(
                jnp.bfloat16
            )
        )
        d_gate_rows = (d_hidden * upper * slope_of(gate)).astype(jnp.bfloat16)
        d_up_rows = (d_hidden * jax.nn.silu(gate)).astype(jnp.bfloat16)
        grad_gate.append(
            jnp.einsum("rh,rd->hd", d_gate_rows, x_rows, preferred_element_type=jnp.float32).astype(
                jnp.bfloat16
            )
        )
        grad_up.append(
            jnp.einsum("rh,rd->hd", d_up_rows, x_rows, preferred_element_type=jnp.float32).astype(
                jnp.bfloat16
            )
        )
        term = jnp.dot(d_gate_rows, gate_exp[local], preferred_element_type=jnp.float32)
        term = term + jnp.dot(d_up_rows, up_exp[local], preferred_element_type=jnp.float32)
        back_terms.append(term)
    d_rows = to_sources(back_terms, n_ep, tcap)
    d_choice = jnp.take(d_rows, slot_ids, axis=0).astype(jnp.float32)
    d_tokens = jnp.sum(d_choice.reshape(tok_dev, TOPK, local_width), 1).astype(jnp.bfloat16)
    return (
        output,
        d_tokens,
        d_weight,
        jnp.stack(grad_gate, 0),
        jnp.stack(grad_up, 0),
        jnp.stack(grad_down, 0),
    )


def solution(mesh):
    in_specs = (
        P("ep", None),
        P("ep", None),
        P(("tp", "ep"), None),
        P(("tp", "ep"), None),
        P(("tp", "ep"), None),
        P(("tp", "ep")),
        P(("tp", "ep")),
        P("ep", None),
        P("ep", None),
    )
    out_specs = (
        P("ep", "tp"),
        P("ep", "tp"),
        P("ep", None),
        P("ep", "tp", None),
        P("ep", "tp", None),
        P("ep", "tp", None),
    )
    return jax.shard_map(body, mesh=mesh, in_specs=in_specs, out_specs=out_specs, check_vma=False)
```

profile of v0, /device:TPU:2, one launch (start us, length us, event | category | flops | bytes accessed | tf_op | source)
XLA Modules:
  0.0 628.7 jit_solution(13298264075085638580)
XLA Ops:
  9.0 11.6 %all-to-all-start.1 = ((bf16[32,1,4]{2,1,0:T(2,128)(2,1)}), bf16[32,1,4]{2,1,0:T(2,128)(2,1)S(1)}, u32[]{:S(2)}, u32[]{:S(2)}) async-start(bf16[32,1,4]{2,1,0:T(2,128)(2,1)} %convert_element_type.135), calls=%async_computation.1 | async-start | bytes 32768 | tf_op jit(solution)/shard_map/all_to_all | solution.py:81
  20.8 3.2 gather_fusion.6
  30.3 5.6 select_select_fusion.2
  35.9 4.1 reshape.188
  40.0 9.8 %all-to-all-start.4 = ((bf16[32,4,8192]{2,1,0:T(4,128)(2,1)}), bf16[32,4,8192]{2,1,0:T(4,128)(2,1)}, u32[]{:S(2)}, u32[]{:S(2)}) async-start(bf16[32,4,8192]{2,1,0:T(4,128)(2,1)} %reshape.188), calls=%async_computation.4 | async-start | bytes 4194304 | tf_op jit(solution)/shard_map/all_to_all | solution.py:80
  49.9 4.1 reshape.186
  54.0 44.7 %all-to-all-done.4 = bf16[32,4,8192]{2,1,0:T(4,128)(2,1)} async-done(((bf16[32,4,8192]{2,1,0:T(4,128)(2,1)}), bf16[32,4,8192]{2,1,0:T(4,128)(2,1)}, u32[]{:S(2)}, u32[]{:S(2)}) %all-to-all-start.4) | async-done | bytes 2097184 | tf_op jit(solution)/shard_map/all_to_all | solution.py:80
  98.7 6.8 %all-to-all-start.3 = ((bf16[32,4,8192]{2,1,0:T(4,128)(2,1)}), bf16[32,4,8192]{2,1,0:T(4,128)(2,1)}, u32[]{:S(2)}, u32[]{:S(2)}) async-start(bf16[32,4,8192]{2,1,0:T(4,128)(2,1)} %reshape.186), calls=%async_computation.3 | async-start | bytes 4194304 | tf_op jit(solution)/shard_map/all_to_all | solution.py:79
  107.7 47.0 %all-to-all-done.3 = bf16[32,4,8192]{2,1,0:T(4,128)(2,1)} async-done(((bf16[32,4,8192]{2,1,0:T(4,128)(2,1)}), bf16[32,4,8192]{2,1,0:T(4,128)(2,1)}, u32[]{:S(2)}, u32[]{:S(2)}) %all-to-all-start.3) | async-done | bytes 2097184 | tf_op jit(solution)/shard_map/all_to_all | solution.py:79
  154.7 5.6 all-to-all-start.2
  161.0 5.2 gather_fusion.9
  166.2 5.1 gather_fusion.1
  173.3 6.2 fusion.9
  179.5 28.3 %all-to-all-done.2 = bf16[32,4,8192]{2,1,0:T(4,128)(2,1)S(1)} async-done(((bf16[32,4,8192]{2,1,0:T(4,128)(2,1)}), bf16[32,4,8192]{2,1,0:T(4,128)(2,1)S(1)}, u32[]{:S(2)}, u32[]{:S(2)}) %all-to-all-start.2) | async-done | bytes 2097184 | tf_op jit(solution)/shard_map/all_to_all | solution.py:78
  207.7 99.2 %all_to_all.41 = bf16[32,8,8192]{2,1,0:T(8,128)(2,1)} all-to-all(bf16[32,8,8192]{2,1,0:T(8,128)(2,1)} %get-tuple-element.51), channel_id=1, replica_groups=mesh['tp'=8,'ep'=32] {'ep'}, dimensions={0} | all-to-all | bytes 8388608 | tf_op jit(solution)/shard_map/all_to_all | solution.py:36
  306.9 5.6 all-to-all-start.6
  330.4 5.9 select_select_fusion.1
  336.3 7.2 %reshape.183 = bf16[32,2,4,8192]{3,2,1,0:T(4,128)(2,1)} reshape(bf16[32,8,8192]{2,1,0:T(8,128)(2,1)} %all_to_all.41) | data formatting | bytes 8388608 | tf_op jit(solution)/shard_map/reshape | solution.py:105
  343.5 5.4 fusion.45
  355.2 49.9 %all-to-all-done.6 = bf16[32,8,8192]{2,1,0:T(8,128)(2,1)} async-done(((bf16[32,8,8192]{2,1,0:T(8,128)(2,1)}), bf16[32,8,8192]{2,1,0:T(8,128)(2,1)}, u32[]{:S(2)}, u32[]{:S(2)}) %all-to-all-start.6) | async-done | bytes 4194336 | tf_op jit(solution)/shard_map/all_to_all | solution.py:36
  405.1 7.2 %reshape.194 = bf16[32,2,4,8192]{3,2,1,0:T(4,128)(2,1)} reshape(bf16[32,8,8192]{2,1,0:T(8,128)(2,1)} %all-to-all-done.6) | data formatting | bytes 8388608 | tf_op jit(solution)/shard_map/reshape | solution.py:133
  412.3 5.4 fusion.44
  417.7 4.1 reshape_squeeze.15
  429.0 3.9 reshape_squeeze.14
  461.0 37.3 %reduce-scatter.5.cloned.1.call-done = bf16[128,1024]{1,0:T(8,128)(2,1)} async-done(((bf16[128,8192]{1,0:T(8,128)(2,1)}), bf16[128,1024]{1,0:T(8,128)(2,1)}) %reduce-scatter.5.cloned.1.call-update) | async-done | bytes 262160 | tf_op jit(solution)/shard_map/reduce_scatter | solution.py:42
  500.7 10.1 %all-to-all-start.5 = ((bf16[32,8,1024]{2,1,0:T(8,128)(2,1)}), bf16[32,8,1024]{2,1,0:T(8,128)(2,1)S(1)}, u32[]{:S(2)}, u32[]{:S(2)}) async-start(bf16[32,8,1024]{2,1,0:T(8,128)(2,1)} %copy.42), calls=%async_computation.7 | async-start | bytes 1048576 | tf_op jit(solution)/shard_map/all_to_all | solution.py:45
  510.8 3.2 pad_maximum_fusion.2
  514.0 23.2 %reduce-scatter.11.cloned.1.call-done = bf16[128,1024]{1,0:T(8,128)(2,1)} async-done(((bf16[128,8192]{1,0:T(8,128)(2,1)}), bf16[128,1024]{1,0:T(8,128)(2,1)}) %reduce-scatter.11.cloned.1.call-update) | async-done | bytes 262160 | tf_op jit(solution)/shard_map/reduce_scatter | solution.py:42
  538.3 36.6 %reduce-scatter.9.cloned.1.call-done = bf16[128,1024]{1,0:T(8,128)(2,1)} async-done(((bf16[128,8192]{1,0:T(8,128)(2,1)}), bf16[128,1024]{1,0:T(8,128)(2,1)}) %reduce-scatter.9.cloned.1.call-update) | async-done | bytes 262160 | tf_op jit(solution)/shard_map/reduce_scatter | solution.py:42
  577.2 10.2 %all-to-all-start.7 = ((bf16[32,8,1024]{2,1,0:T(8,128)(2,1)}), bf16[32,8,1024]{2,1,0:T(8,128)(2,1)}, u32[]{:S(2)}, u32[]{:S(2)}) async-start(bf16[32,8,1024]{2,1,0:T(8,128)(2,1)} %copy.45), calls=%async_computation.11 | async-start | bytes 1048576 | tf_op jit(solution)/shard_map/all_to_all | solution.py:45
  592.5 9.1 %all-to-all-done.7 = bf16[32,8,1024]{2,1,0:T(8,128)(2,1)} async-done(((bf16[32,8,1024]{2,1,0:T(8,128)(2,1)}), bf16[32,8,1024]{2,1,0:T(8,128)(2,1)}, u32[]{:S(2)}, u32[]{:S(2)}) %all-to-all-start.7) | async-done | bytes 524320 | tf_op jit(solution)/shard_map/all_to_all | solution.py:45
  605.8 15.7 %psum.7 = f32[16,8]{1,0:T(8,128)S(1)} all-reduce(f32[16,8]{1,0:T(8,128)S(1)} %reduce_sum.95), channel_id=1, replica_groups=mesh['tp'=8,'ep'=32] {'tp'}, use_global_device_ids=true, to_apply=%region_16.21 | all-reduce | flops 128 | bytes 1024 | tf_op jit(solution)/shard_map/psum | solution.py:127
  (142 shorter events, 87.9 us)
Async XLA Ops:
  7.2 13.6 %copy-start = (bf16[56,8192]{1,0:T(8,128)(2,1)S(1)}, bf16[56,8192]{1,0:T(8,128)(2,1)}, u32[]{:S(2)}) copy-start(bf16[56,8192]{1,0:T(8,128)(2,1)} %param.21) | copy-start | bytes 2752516
  9.0 31.1 %all-to-all-start.1 = ((bf16[32,1,4]{2,1,0:T(2,128)(2,1)}), bf16[32,1,4]{2,1,0:T(2,128)(2,1)S(1)}, u32[]{:S(2)}, u32[]{:S(2)}) async-start(bf16[32,1,4]{2,1,0:T(2,128)(2,1)} %convert_element_type.135), calls=%async_computation.1 | async-start | bytes 32768 | tf_op jit(solution)/shard_map/all_to_all | solution.py:81
  20.7 3.2 copy-start.4
  23.9 3.2 copy-start.5
  40.0 58.7 %all-to-all-start.4 = ((bf16[32,4,8192]{2,1,0:T(4,128)(2,1)}), bf16[32,4,8192]{2,1,0:T(4,128)(2,1)}, u32[]{:S(2)}, u32[]{:S(2)}) async-start(bf16[32,4,8192]{2,1,0:T(4,128)(2,1)} %reshape.188), calls=%async_computation.4 | async-start | bytes 4194304 | tf_op jit(solution)/shard_map/all_to_all | solution.py:80
  98.7 56.0 %all-to-all-start.3 = ((bf16[32,4,8192]{2,1,0:T(4,128)(2,1)}), bf16[32,4,8192]{2,1,0:T(4,128)(2,1)}, u32[]{:S(2)}, u32[]{:S(2)}) async-start(bf16[32,4,8192]{2,1,0:T(4,128)(2,1)} %reshape.186), calls=%async_computation.3 | async-start | bytes 4194304 | tf_op jit(solution)/shard_map/all_to_all | solution.py:79
  107.7 52.5 %copy-start.22 = (f32[16,8]{0,1:T(8,128)S(1)}, f32[16,8]{0,1:T(8,128)}, u32[]{:S(2)}) copy-start(f32[16,8]{0,1:T(8,128)} %param.25) | copy-start | bytes 1540
  107.7 52.7 %copy-start.23 = (s32[16,8]{0,1:T(8,128)S(1)}, s32[16,8]{0,1:T(8,128)}, u32[]{:S(2)}) copy-start(s32[16,8]{0,1:T(8,128)} %param.24) | copy-start | bytes 1540
  107.7 53.2 %copy-start.2 = (bf16[16,8192]{1,0:T(8,128)(2,1)S(1)}, bf16[16,8192]{1,0:T(8,128)(2,1)}, u32[]{:S(2)}) copy-start(bf16[16,8192]{1,0:T(8,128)(2,1)} %param.18) | copy-start | bytes 786436
  154.7 53.0 %all-to-all-start.2 = ((bf16[32,4,8192]{2,1,0:T(4,128)(2,1)}), bf16[32,4,8192]{2,1,0:T(4,128)(2,1)S(1)}, u32[]{:S(2)}, u32[]{:S(2)}) async-start(bf16[32,4,8192]{2,1,0:T(4,128)(2,1)} %reshape.184), calls=%async_computation.2 | async-start | bytes 4194304 | tf_op jit(solution)/shard_map/all_to_all | solution.py:78
  161.0 5.2 copy-start.3
  207.7 99.2 %copy-start.17 = (bf16[32,4,8192]{2,1,0:T(4,128)(2,1)}, bf16[32,4,8192]{2,1,0:T(4,128)(2,1)S(1)}, u32[]{:S(2)}) copy-start(bf16[32,4,8192]{2,1,0:T(4,128)(2,1)S(1)} %all-to-all-done.2) | copy-start | bytes 6291460
  306.9 98.2 %all-to-all-start.6 = ((bf16[32,8,8192]{2,1,0:T(8,128)(2,1)}), bf16[32,8,8192]{2,1,0:T(8,128)(2,1)}, u32[]{:S(2)}, u32[]{:S(2)}) async-start(bf16[32,8,8192]{2,1,0:T(8,128)(2,1)} %get-tuple-element.50), calls=%async_computation.8 | async-start | bytes 8388608 | tf_op jit(solution)/shard_map/all_to_all | solution.py:36
  312.5 147.4 %reduce-scatter.7.cloned.1.call-start = ((), (), s32[]{:S(2)}) async-start(), calls=%async_computation.13 | async-start | bytes 2359296 | tf_op jit(solution)/shard_map/reduce_scatter | solution.py:42
  351.4 3.8 copy-start.6
  351.4 2.9 copy-start.8
  417.7 4.1 copy-start.12
  426.4 72.0 %reduce-scatter.5.cloned.1.call-start = ((), (), s32[]{:S(2)}) async-start(), calls=%async_computation.12 | async-start | bytes 2359296 | tf_op jit(solution)/shard_map/reduce_scatter | solution.py:42
  432.9 2.3 copy-start.9
  432.9 3.1 copy-start.15
  439.8 97.4 %reduce-scatter.11.cloned.1.call-start = ((), (), s32[]{:S(2)}) async-start(), calls=%async_computation.15 | async-start | bytes 2359296 | tf_op jit(solution)/shard_map/reduce_scatter | solution.py:42
  440.1 2.1 copy-start.10
  444.3 130.6 %reduce-scatter.9.cloned.1.call-start = ((), (), s32[]{:S(2)}) async-start(), calls=%async_computation.14 | async-start | bytes 2359296 | tf_op jit(solution)/shard_map/reduce_scatter | solution.py:42
  444.4 2.1 copy-start.11
  452.3 2.0 copy-start.7
  454.3 2.0 copy-start.14
  456.3 2.0 copy-start.16
  500.7 76.6 %all-to-all-start.5 = ((bf16[32,8,1024]{2,1,0:T(8,128)(2,1)}), bf16[32,8,1024]{2,1,0:T(8,128)(2,1)S(1)}, u32[]{:S(2)}, u32[]{:S(2)}) async-start(bf16[32,8,1024]{2,1,0:T(8,128)(2,1)} %copy.42), calls=%async_computation.7 | async-start | bytes 1048576 | tf_op jit(solution)/shard_map/all_to_all | solution.py:45
  577.2 24.3 %all-to-all-start.7 = ((bf16[32,8,1024]{2,1,0:T(8,128)(2,1)}), bf16[32,8,1024]{2,1,0:T(8,128)(2,1)}, u32[]{:S(2)}, u32[]{:S(2)}) async-start(bf16[32,8,1024]{2,1,0:T(8,128)(2,1)} %copy.45), calls=%async_computation.11 | async-start | bytes 1048576 | tf_op jit(solution)/shard_map/all_to_all | solution.py:45
  587.4 1.8 copy-start.20
  591.7 13.8 %copy-start.21 = (f32[16,1024]{1,0:T(8,128)S(1)}, f32[16,1024]{1,0:T(8,128)}, u32[]{:S(2)}) copy-start(f32[16,1024]{1,0:T(8,128)} %dynamic-slice_convert_fusion) | copy-start | bytes 196612
  591.7 30.5 %copy-start.1 = (bf16[56,8192]{1,0:T(8,128)(2,1)S(1)}, bf16[56,8192]{1,0:T(8,128)(2,1)}, u32[]{:S(2)}) copy-start(bf16[56,8192]{1,0:T(8,128)(2,1)} %param.21) | copy-start | bytes 2752516
  (3 other events, 4.5 us)
Sparse Core Ops, SparseCore 0:
  426.5 33.3 reduce-scatter.6
  463.0 35.3 reduce-scatter.4
  501.5 35.6 reduce-scatter.10
  539.6 35.2 reduce-scatter.8
where the time goes:
time: 631 us; the launch traced here: 629 us
  waiting for transfers between devices  276 us (44%)
  blocking collectives  115 us (18%)
  local copies, waits for them, and re-layouts  103 us (16%)
  starting transfers between devices  60.4 us (10%)
  matrix products  31.7 us (5%)
  other arithmetic  27.9 us (4%)
  between operations  14.3 us (2%)
    all_to_all x1, blocking collectives, dispatch(): return lax.all_to_all(rows, 'ep', split_axis=0, concat_axis=0, tiled=True)  99.2 us
    reduce_scatter x4, waiting for transfers between devices, to_sources(): lax.psum_scatter(term.astype(jnp.bfloat16), 'tp', scatter_dimension=1, ti...  97.3 us
    all_to_all x1, waiting for transfers between devices, dispatch(): return lax.all_to_all(rows, 'ep', split_axis=0, concat_axis=0, tiled=True)  49.9 us
    all_to_all x1, waiting for transfers between devices, body(): lax.all_to_all(pack(w_up), 'ep', split_axis=0, concat_axis=0, tiled=True)  47 us
    all_to_all x1, waiting for transfers between devices, body(): lax.all_to_all(pack(w_down), 'ep', split_axis=0, concat_axis=0, tiled=True)  44.7 us
    all_to_all x1, waiting for transfers between devices, body(): lax.all_to_all(pack(w_gate), 'ep', split_axis=0, concat_axis=0, tiled=True)  28.3 us
    gather x7, local copies, waits for them, and re-layouts, pick_rows(): taken = jnp.take(rows, index, axis=0)  24.2 us
    all_to_all x2, starting transfers between devices, to_sources(): lax.all_to_all(stacked, 'ep', split_axis=0, concat_axis=0, tiled=True)  20.3 us
  transfers between devices with their start and end apart: 11, of which 9 were waited for; matrix products, arithmetic and copies ran while one was open for 21% of the time, Pallas kernels for 0%

commit v1 on v0

--- a/solution.py
+++ b/solution.py
@@ -124,7 +124,7 @@
     partial_value = jnp.sum(
         per_choice.reshape(tok_dev, TOPK, local_width) * cot_local[:, None, :], 2
     )
-    d_weight = lax.psum(partial_value, "tp")
+    d_weight = jnp.sum(lax.all_gather(partial_value, "tp"), axis=0)
     slot_weight = jnp.take(choice_weight.reshape(-1), choice_of_slot, axis=0)
     slot_cot = jnp.take(cotangent, choice_of_slot // TOPK, axis=0).astype(jnp.float32)
     scaled_rows = (slot_weight[:, None] * slot_cot).astype(jnp.bfloat16)

time: 631 us -> 636 us (level); the launches traced: 629 us -> 626 us
    psum x1 -> x0, blocking collectives: 15.7 us -> none  [body(): d_weight = lax.psum(partial_value, 'tp')]
    all_gather x0 -> x1, blocking collectives: none -> 13.1 us  [body(): d_weight = jnp.sum(lax.all_gather(partial_value, 'tp'), axis=0)]
where the time goes in v1:
time: 636 us; the launch traced here: 626 us
  waiting for transfers between devices  276 us (43%)
  blocking collectives  112 us (18%)
  local copies, waits for them, and re-layouts  103 us (16%)
  starting transfers between devices  60.8 us (10%)
  matrix products  31.7 us (5%)
  other arithmetic  28.5 us (4%)
  between operations  14.5 us (2%)
    all_to_all x1, blocking collectives, dispatch(): return lax.all_to_all(rows, 'ep', split_axis=0, concat_axis=0, tiled=True)  99.2 us
    reduce_scatter x4, waiting for transfers between devices, to_sources(): lax.psum_scatter(term.astype(jnp.bfloat16), 'tp', scatter_dimension=1, ti...  97.1 us
    all_to_all x1, waiting for transfers between devices, dispatch(): return lax.all_to_all(rows, 'ep', split_axis=0, concat_axis=0, tiled=True)  50 us
    all_to_all x1, waiting for transfers between devices, body(): lax.all_to_all(pack(w_up), 'ep', split_axis=0, concat_axis=0, tiled=True)  47 us
    all_to_all x1, waiting for transfers between devices, body(): lax.all_to_all(pack(w_down), 'ep', split_axis=0, concat_axis=0, tiled=True)  44.7 us
    all_to_all x1, waiting for transfers between devices, body(): lax.all_to_all(pack(w_gate), 'ep', split_axis=0, concat_axis=0, tiled=True)  28.2 us
    gather x7, local copies, waits for them, and re-layouts, pick_rows(): taken = jnp.take(rows, index, axis=0)  24.2 us
    all_to_all x2, starting transfers between devices, to_sources(): lax.all_to_all(stacked, 'ep', split_axis=0, concat_axis=0, tiled=True)  20.2 us
  transfers between devices with their start and end apart: 11, of which 9 were waited for; matrix products, arithmetic and copies ran while one was open for 21% of the time, Pallas kernels for 0%

profile of v1, /device:TPU:2, one launch (start us, length us, event | category | flops | bytes accessed | tf_op | source)
XLA Modules:
  0.0 626.5 jit_solution(1794479664540960971)
XLA Ops:
  9.0 11.6 %all-to-all-start.1 = ((bf16[32,1,4]{2,1,0:T(2,128)(2,1)}), bf16[32,1,4]{2,1,0:T(2,128)(2,1)S(1)}, u32[]{:S(2)}, u32[]{:S(2)}) async-start(bf16[32,1,4]{2,1,0:T(2,128)(2,1)} %convert_element_type.135), calls=%async_computation.1 | async-start | bytes 32768 | tf_op jit(solution)/shard_map/all_to_all | solution.py:81
  30.3 5.6 select_select_fusion.2
  35.9 4.1 reshape.189
  40.0 9.8 %all-to-all-start.4 = ((bf16[32,4,8192]{2,1,0:T(4,128)(2,1)}), bf16[32,4,8192]{2,1,0:T(4,128)(2,1)}, u32[]{:S(2)}, u32[]{:S(2)}) async-start(bf16[32,4,8192]{2,1,0:T(4,128)(2,1)} %reshape.189), calls=%async_computation.4 | async-start | bytes 4194304 | tf_op jit(solution)/shard_map/all_to_all | solution.py:80
  49.9 4.1 reshape.187
  54.0 44.7 %all-to-all-done.4 = bf16[32,4,8192]{2,1,0:T(4,128)(2,1)} async-done(((bf16[32,4,8192]{2,1,0:T(4,128)(2,1)}), bf16[32,4,8192]{2,1,0:T(4,128)(2,1)}, u32[]{:S(2)}, u32[]{:S(2)}) %all-to-all-start.4) | async-done | bytes 2097184 | tf_op jit(solution)/shard_map/all_to_all | solution.py:80
  98.7 6.8 %all-to-all-start.3 = ((bf16[32,4,8192]{2,1,0:T(4,128)(2,1)}), bf16[32,4,8192]{2,1,0:T(4,128)(2,1)}, u32[]{:S(2)}, u32[]{:S(2)}) async-start(bf16[32,4,8192]{2,1,0:T(4,128)(2,1)} %reshape.187), calls=%async_computation.3 | async-start | bytes 4194304 | tf_op jit(solution)/shard_map/all_to_all | solution.py:79
  107.7 47.0 %all-to-all-done.3 = bf16[32,4,8192]{2,1,0:T(4,128)(2,1)} async-done(((bf16[32,4,8192]{2,1,0:T(4,128)(2,1)}), bf16[32,4,8192]{2,1,0:T(4,128)(2,1)}, u32[]{:S(2)}, u32[]{:S(2)}) %all-to-all-start.3) | async-done | bytes 2097184 | tf_op jit(solution)/shard_map/all_to_all | solution.py:79
  154.7 6.1 all-to-all-start.2
  161.6 5.2 gather_fusion.9
  166.7 5.1 gather_fusion.1
  173.9 6.2 fusion.9
  180.0 28.2 %all-to-all-done.2 = bf16[32,4,8192]{2,1,0:T(4,128)(2,1)S(1)} async-done(((bf16[32,4,8192]{2,1,0:T(4,128)(2,1)}), bf16[32,4,8192]{2,1,0:T(4,128)(2,1)S(1)}, u32[]{:S(2)}, u32[]{:S(2)}) %all-to-all-start.2) | async-done | bytes 2097184 | tf_op jit(solution)/shard_map/all_to_all | solution.py:78
  208.2 99.2 %all_to_all.41 = bf16[32,8,8192]{2,1,0:T(8,128)(2,1)} all-to-all(bf16[32,8,8192]{2,1,0:T(8,128)(2,1)} %get-tuple-element.39), channel_id=1, replica_groups=mesh['tp'=8,'ep'=32] {'ep'}, dimensions={0} | all-to-all | bytes 8388608 | tf_op jit(solution)/shard_map/all_to_all | solution.py:36
  307.4 5.6 all-to-all-start.6
  327.7 3.2 gather_fusion.3
  330.8 5.9 select_select_fusion.1
  336.7 7.2 %reshape.184 = bf16[32,2,4,8192]{3,2,1,0:T(4,128)(2,1)} reshape(bf16[32,8,8192]{2,1,0:T(8,128)(2,1)} %all_to_all.41) | data formatting | bytes 8388608 | tf_op jit(solution)/shard_map/reshape | solution.py:105
  343.9 5.4 fusion.45
  355.6 50.0 %all-to-all-done.6 = bf16[32,8,8192]{2,1,0:T(8,128)(2,1)} async-done(((bf16[32,8,8192]{2,1,0:T(8,128)(2,1)}), bf16[32,8,8192]{2,1,0:T(8,128)(2,1)}, u32[]{:S(2)}, u32[]{:S(2)}) %all-to-all-start.6) | async-done | bytes 4194336 | tf_op jit(solution)/shard_map/all_to_all | solution.py:36
  405.6 7.2 %reshape.195 = bf16[32,2,4,8192]{3,2,1,0:T(4,128)(2,1)} reshape(bf16[32,8,8192]{2,1,0:T(8,128)(2,1)} %all-to-all-done.6) | data formatting | bytes 8388608 | tf_op jit(solution)/shard_map/reshape | solution.py:133
  412.8 5.4 fusion.44
  418.2 4.1 reshape_squeeze.15
  429.4 3.9 reshape_squeeze.14
  461.5 37.2 %reduce-scatter.5.cloned.1.call-done = bf16[128,1024]{1,0:T(8,128)(2,1)} async-done(((bf16[128,8192]{1,0:T(8,128)(2,1)}), bf16[128,1024]{1,0:T(8,128)(2,1)}) %reduce-scatter.5.cloned.1.call-update) | async-done | bytes 262160 | tf_op jit(solution)/shard_map/reduce_scatter | solution.py:42
  501.0 10.1 %all-to-all-start.5 = ((bf16[32,8,1024]{2,1,0:T(8,128)(2,1)}), bf16[32,8,1024]{2,1,0:T(8,128)(2,1)S(1)}, u32[]{:S(2)}, u32[]{:S(2)}) async-start(bf16[32,8,1024]{2,1,0:T(8,128)(2,1)} %copy.42), calls=%async_computation.7 | async-start | bytes 1048576 | tf_op jit(solution)/shard_map/all_to_all | solution.py:45
  511.1 3.2 pad_maximum_fusion.2
  514.3 23.2 %reduce-scatter.11.cloned.1.call-done = bf16[128,1024]{1,0:T(8,128)(2,1)} async-done(((bf16[128,8192]{1,0:T(8,128)(2,1)}), bf16[128,1024]{1,0:T(8,128)(2,1)}) %reduce-scatter.11.cloned.1.call-update) | async-done | bytes 262160 | tf_op jit(solution)/shard_map/reduce_scatter | solution.py:42
  538.6 36.5 %reduce-scatter.9.cloned.1.call-done = bf16[128,1024]{1,0:T(8,128)(2,1)} async-done(((bf16[128,8192]{1,0:T(8,128)(2,1)}), bf16[128,1024]{1,0:T(8,128)(2,1)}) %reduce-scatter.9.cloned.1.call-update) | async-done | bytes 262160 | tf_op jit(solution)/shard_map/reduce_scatter | solution.py:42
  577.4 10.1 %all-to-all-start.7 = ((bf16[32,8,1024]{2,1,0:T(8,128)(2,1)}), bf16[32,8,1024]{2,1,0:T(8,128)(2,1)}, u32[]{:S(2)}, u32[]{:S(2)}) async-start(bf16[32,8,1024]{2,1,0:T(8,128)(2,1)} %copy.45), calls=%async_computation.11 | async-start | bytes 1048576 | tf_op jit(solution)/shard_map/all_to_all | solution.py:45
  592.7 9.0 %all-to-all-done.7 = bf16[32,8,1024]{2,1,0:T(8,128)(2,1)} async-done(((bf16[32,8,1024]{2,1,0:T(8,128)(2,1)}), bf16[32,8,1024]{2,1,0:T(8,128)(2,1)}, u32[]{:S(2)}, u32[]{:S(2)}) %all-to-all-start.7) | async-done | bytes 524320 | tf_op jit(solution)/shard_map/all_to_all | solution.py:45
  605.9 13.1 %all_gather.7 = f32[8,16,8]{1,2,0:T(8,128)S(1)} all-gather(f32[1,16,8]{1,2,0:T(8,128)S(1)} %copy.46), channel_id=1, replica_groups=mesh['tp'=8,'ep'=32] {'tp'}, dimensions={0}, use_global_device_ids=true | all-gather | bytes 4608 | tf_op jit(solution)/shard_map/all_gather | solution.py:127
  (143 shorter events, 87.9 us)
Async XLA Ops:
  7.2 13.6 %copy-start = (bf16[56,8192]{1,0:T(8,128)(2,1)S(1)}, bf16[56,8192]{1,0:T(8,128)(2,1)}, u32[]{:S(2)}) copy-start(bf16[56,8192]{1,0:T(8,128)(2,1)} %param.21) | copy-start | bytes 2752516
  9.0 31.1 %all-to-all-start.1 = ((bf16[32,1,4]{2,1,0:T(2,128)(2,1)}), bf16[32,1,4]{2,1,0:T(2,128)(2,1)S(1)}, u32[]{:S(2)}, u32[]{:S(2)}) async-start(bf16[32,1,4]{2,1,0:T(2,128)(2,1)} %convert_element_type.135), calls=%async_computation.1 | async-start | bytes 32768 | tf_op jit(solution)/shard_map/all_to_all | solution.py:81
  20.7 3.2 copy-start.4
  23.9 3.2 copy-start.5
  40.0 58.7 %all-to-all-start.4 = ((bf16[32,4,8192]{2,1,0:T(4,128)(2,1)}), bf16[32,4,8192]{2,1,0:T(4,128)(2,1)}, u32[]{:S(2)}, u32[]{:S(2)}) async-start(bf16[32,4,8192]{2,1,0:T(4,128)(2,1)} %reshape.189), calls=%async_computation.4 | async-start | bytes 4194304 | tf_op jit(solution)/shard_map/all_to_all | solution.py:80
  98.7 56.0 %all-to-all-start.3 = ((bf16[32,4,8192]{2,1,0:T(4,128)(2,1)}), bf16[32,4,8192]{2,1,0:T(4,128)(2,1)}, u32[]{:S(2)}, u32[]{:S(2)}) async-start(bf16[32,4,8192]{2,1,0:T(4,128)(2,1)} %reshape.187), calls=%async_computation.3 | async-start | bytes 4194304 | tf_op jit(solution)/shard_map/all_to_all | solution.py:79
  107.7 53.1 %copy-start.22 = (f32[16,8]{0,1:T(8,128)S(1)}, f32[16,8]{0,1:T(8,128)}, u32[]{:S(2)}) copy-start(f32[16,8]{0,1:T(8,128)} %param.25) | copy-start | bytes 1540
  107.7 53.3 %copy-start.23 = (s32[16,8]{0,1:T(8,128)S(1)}, s32[16,8]{0,1:T(8,128)}, u32[]{:S(2)}) copy-start(s32[16,8]{0,1:T(8,128)} %param.24) | copy-start | bytes 1540
  107.7 53.8 %copy-start.2 = (bf16[16,8192]{1,0:T(8,128)(2,1)S(1)}, bf16[16,8192]{1,0:T(8,128)(2,1)}, u32[]{:S(2)}) copy-start(bf16[16,8192]{1,0:T(8,128)(2,1)} %param.18) | copy-start | bytes 786436
  154.7 53.5 %all-to-all-start.2 = ((bf16[32,4,8192]{2,1,0:T(4,128)(2,1)}), bf16[32,4,8192]{2,1,0:T(4,128)(2,1)S(1)}, u32[]{:S(2)}, u32[]{:S(2)}) async-start(bf16[32,4,8192]{2,1,0:T(4,128)(2,1)} %reshape.185), calls=%async_computation.2 | async-start | bytes 4194304 | tf_op jit(solution)/shard_map/all_to_all | solution.py:78
  161.6 5.2 copy-start.3
  208.2 99.2 %copy-start.17 = (bf16[32,4,8192]{2,1,0:T(4,128)(2,1)}, bf16[32,4,8192]{2,1,0:T(4,128)(2,1)S(1)}, u32[]{:S(2)}) copy-start(bf16[32,4,8192]{2,1,0:T(4,128)(2,1)S(1)} %all-to-all-done.2) | copy-start | bytes 6291460
  307.4 98.2 %all-to-all-start.6 = ((bf16[32,8,8192]{2,1,0:T(8,128)(2,1)}), bf16[32,8,8192]{2,1,0:T(8,128)(2,1)}, u32[]{:S(2)}, u32[]{:S(2)}) async-start(bf16[32,8,8192]{2,1,0:T(8,128)(2,1)} %get-tuple-element.38), calls=%async_computation.8 | async-start | bytes 8388608 | tf_op jit(solution)/shard_map/all_to_all | solution.py:36
  313.0 147.4 %reduce-scatter.7.cloned.1.call-start = ((), (), s32[]{:S(2)}) async-start(), calls=%async_computation.13 | async-start | bytes 2359296 | tf_op jit(solution)/shard_map/reduce_scatter | solution.py:42
  351.8 3.8 copy-start.6
  351.8 2.9 copy-start.8
  418.2 4.1 copy-start.12
  426.8 71.9 %reduce-scatter.5.cloned.1.call-start = ((), (), s32[]{:S(2)}) async-start(), calls=%async_computation.12 | async-start | bytes 2359296 | tf_op jit(solution)/shard_map/reduce_scatter | solution.py:42
  433.4 2.3 copy-start.9
  433.4 3.1 copy-start.15
  440.3 97.2 %reduce-scatter.11.cloned.1.call-start = ((), (), s32[]{:S(2)}) async-start(), calls=%async_computation.15 | async-start | bytes 2359296 | tf_op jit(solution)/shard_map/reduce_scatter | solution.py:42
  440.5 2.1 copy-start.10
  444.7 130.4 %reduce-scatter.9.cloned.1.call-start = ((), (), s32[]{:S(2)}) async-start(), calls=%async_computation.14 | async-start | bytes 2359296 | tf_op jit(solution)/shard_map/reduce_scatter | solution.py:42
  444.8 2.1 copy-start.11
  452.7 2.0 copy-start.7
  454.7 2.0 copy-start.14
  456.7 2.0 copy-start.16
  501.0 76.4 %all-to-all-start.5 = ((bf16[32,8,1024]{2,1,0:T(8,128)(2,1)}), bf16[32,8,1024]{2,1,0:T(8,128)(2,1)S(1)}, u32[]{:S(2)}, u32[]{:S(2)}) async-start(bf16[32,8,1024]{2,1,0:T(8,128)(2,1)} %copy.42), calls=%async_computation.7 | async-start | bytes 1048576 | tf_op jit(solution)/shard_map/all_to_all | solution.py:45
  577.4 24.3 %all-to-all-start.7 = ((bf16[32,8,1024]{2,1,0:T(8,128)(2,1)}), bf16[32,8,1024]{2,1,0:T(8,128)(2,1)}, u32[]{:S(2)}, u32[]{:S(2)}) async-start(bf16[32,8,1024]{2,1,0:T(8,128)(2,1)} %copy.45), calls=%async_computation.11 | async-start | bytes 1048576 | tf_op jit(solution)/shard_map/all_to_all | solution.py:45
  587.6 1.8 copy-start.20
  591.8 13.8 %copy-start.21 = (f32[16,1024]{1,0:T(8,128)S(1)}, f32[16,1024]{1,0:T(8,128)}, u32[]{:S(2)}) copy-start(f32[16,1024]{1,0:T(8,128)} %dynamic-slice_convert_fusion) | copy-start | bytes 196612
  591.8 27.9 %copy-start.1 = (bf16[56,8192]{1,0:T(8,128)(2,1)S(1)}, bf16[56,8192]{1,0:T(8,128)(2,1)}, u32[]{:S(2)}) copy-start(bf16[56,8192]{1,0:T(8,128)(2,1)} %param.21) | copy-start | bytes 2752516
  (3 other events, 4.5 us)
Sparse Core Ops, SparseCore 0:
  426.9 33.3 reduce-scatter.6
  463.5 35.2 reduce-scatter.4
  501.9 35.5 reduce-scatter.10
  539.9 35.2 reduce-scatter.8
